TPU v7x, 32 devices: a whole 2x2x4 slice. The times are simulated.
32 devices in a mesh: dp: 8 (over z, core), mp: 4 (over y, x).
Axes of the slice: x: 2, y: 2, z: 4, core: 2. Of those that a mesh axis runs over, the one named last changes fastest.
Arguments:
- activations: bfloat16 [4096, 8192], P('dp', 'mp')
- value_grad: bfloat16 [4096, 1024], P('dp'), may hold values from -6 to 6
- master: float32 [8192, 1024], P(('mp', 'dp')), may hold values from -6 to 6
- first_moment: float32 [8192, 1024], P(('mp', 'dp')), may hold values from -2 to 2
- second_moment: float32 [8192, 1024], P(('mp', 'dp')), may hold values from 0.05 to 1
- step_count: int32 [1], replicated, may hold values from 1 to 40
Outputs:
- new_master: float32 [8192, 1024], P(('mp', 'dp'))
- new_first: float32 [8192, 1024], P(('mp', 'dp'))
- new_second: float32 [8192, 1024], P(('mp', 'dp'))
- rollout_update: bfloat16 [8192, 1024], P(None, 'mp')
Inputs may be any that keep to these rules, and one draw needn't show every extreme that they name: `step_count`: the number of optimizer steps taken so far, this one included.
All inputs are finite; a program needn't handle non-finite values.
Results may differ from a plain program's by a relative error of at most 0.0004.
Values may be sent and summed in bfloat16 or wider, within the bound.
A program may use at most 64 MiB of HBM per device.

v0:
```python
import math

import jax
import jax.numpy as jnp
from jax import lax
from jax.sharding import PartitionSpec as P

D = 8192
KV = 1024


def on_device(activations, value_grad, master, first_moment, second_moment, step_count):
    own_rows = master.shape[0]
    grad = lax.psum_scatter(
        lax.dot_general(
            activations, value_grad, (((0,), (0,)), ((), ())), preferred_element_type=jnp.float32
        ),
        "dp",
        scatter_dimension=0,
        tiled=True,
    )
    square_sum = lax.psum(jnp.sum(grad * grad), ("dp", "mp"))
    clip_total = 0.5 * math.sqrt(D * KV)
    factor = jnp.minimum(jnp.float32(1.0), clip_total / (jnp.sqrt(square_sum) + 1e-06))
    clipped = factor * grad
    new_first = 0.9 * first_moment + 0.1 * clipped
    new_second = 0.95 * second_moment + 0.05 * clipped * clipped
    steps_done = step_count[0].astype(jnp.float32)
    bias_first = 1.0 - jnp.exp(steps_done * jnp.log(jnp.float32(0.9)))
    bias_second = 1.0 - jnp.exp(steps_done * jnp.log(jnp.float32(0.95)))
    direction = new_first / bias_first / (jnp.sqrt(new_second / bias_second) + 1e-08) + 0.1 * master
    new_master = master - 0.01 * direction
    update = direction.astype(jnp.bfloat16)
    head_count = lax.axis_size("mp")
    received = lax.all_to_all(update, "mp", split_axis=1, concat_axis=0, tiled=True)
    stacked = received.reshape(head_count, own_rows, received.shape[1])
    gathered = lax.all_gather(stacked, "dp", axis=1, tiled=True)
    rollout_update = gathered.reshape(-1, gathered.shape[2])
    return (new_master, new_first, new_second, rollout_update)


def solution(mesh):
    in_specs = (
        P("dp", "mp"),
        P("dp", None),
        P(("mp", "dp"), None),
        P(("mp", "dp"), None),
        P(("mp", "dp"), None),
        P(),
    )
    out_specs = (P(("mp", "dp"), None), P(("mp", "dp"), None), P(("mp", "dp"), None), P(None, "mp"))
    return jax.shard_map(
        on_device, mesh=mesh, in_specs=in_specs, out_specs=out_specs, check_vma=False
    )
```

profile of v0, /device:TPU:0, one launch (start us, length us, event | category | flops | bytes accessed | tf_op | source)
XLA Modules:
  0.0 223.1 jit_solution(2057952666039713074)
XLA Ops:
  7.2 0.0 copy-start
  7.2 0.0 reduce-scatter.2.cloned.1.call-start
  7.2 1.5 copy-done
  8.8 6.8 %fusion.3 = f32[2048,1024]{1,0:T(8,128)} fusion(bf16[512,2048]{1,0:T(8,128)(2,1)S(1)} %copy-done, bf16[512,1024]{1,0:T(8,128)(2,1)} %param.7), kind=kOutput, calls=%fused_computation.8 | convolution fusion | flops 2147483648 | bytes 11534336 | tf_op jit(solution)/shard_map/dot_general | solution.py:15
  15.6 0.0 copy-start.1
  15.6 0.0 reduce-scatter.2.cloned.1.call-update
  15.6 0.0 all-gather.2.cloned.1.call-start
  16.5 91.5 %reduce-scatter.2.cloned.1.call-done = f32[256,1024]{1,0:T(8,128)} async-done(((f32[2048,1024]{1,0:T(8,128)}), f32[256,1024]{1,0:T(8,128)}) %reduce-scatter.2.cloned.1.call-update) | async-done | bytes 1048592 | tf_op jit(solution)/shard_map/reduce_scatter | solution.py:14
  108.0 2.1 multiply_reduce_fusion
  110.1 37.9 %psum.7 = f32[]{:T(128)} all-reduce(f32[]{:T(128)} %multiply_reduce_fusion), channel_id=1, replica_groups=mesh['dp'=8,'mp'=4] {'dp','mp'}, use_global_device_ids=true, to_apply=%region_2.0 | all-reduce | flops 1 | bytes 8 | tf_op jit(solution)/shard_map/psum | solution.py:22
  148.8 0.0 copy-done.1
  148.8 4.1 %fusion.1 = (bf16[256,1024]{1,0:T(8,128)(2,1)S(1)}, f32[256,1024]{1,0:T(8,128)}, f32[256,1024]{1,0:T(8,128)}, f32[256,1024]{1,0:T(8,128)}) fusion(f32[256,1024]{1,0:T(8,128)S(1)} %copy-done.1, f32[]{:T(128)} %bitcast.1, f32[]{:T(128)} %bitcast, f32[256,1024]{1,0:T(8,128)} %reduce-scatter.2.cloned.1.call-done, f32[]{:T(128)S(6)} %min.3, ...), kind=kLoop, calls=%fused_computation.7 | loop fusion | flops 3932160 | bytes 7864332 | tf_op jit(solution)/shard_map/convert_element_type | solution.py:33
  153.0 11.2 %all_to_all.16 = bf16[256,4,256]{2,0,1:T(8,128)(2,1)S(1)} all-to-all(bf16[256,4,256]{2,0,1:T(8,128)(2,1)S(1)} %bitcast.12), channel_id=1, replica_groups=mesh['dp'=8,'mp'=4] {'mp'}, dimensions={1} | all-to-all | bytes 1048576 | tf_op jit(solution)/shard_map/all_to_all | solution.py:35
  164.2 1.2 copy.14
  165.4 0.0 all-gather.2.cloned.1.call-update
  165.4 2.4 %multiply_subtract_fusion = f32[256,1024]{1,0:T(8,128)} fusion(f32[256,1024]{1,0:T(8,128)S(1)} %copy-done.1, f32[256,1024]{1,0:T(8,128)} %get-tuple-element.5), kind=kLoop, calls=%fused_computation.2 | loop fusion | flops 524288 | bytes 3145728 | tf_op jit(solution)/shard_map/sub | solution.py:32
  167.8 43.7 %all-gather.2.cloned.1.call-done = bf16[4,2048,256]{2,0,1:T(4,128)(2,1)} async-done(((bf16[4,256,256]{2,0,1:T(4,128)(2,1)}), bf16[4,2048,256]{2,0,1:T(4,128)(2,1)}) %all-gather.2.cloned.1.call-update) | async-done | bytes 4194320 | tf_op jit(solution)/shard_map/all_gather | solution.py:37
  211.5 4.7 %copy.15 = bf16[4,2048,256]{2,1,0:T(8,128)(2,1)} copy(bf16[4,2048,256]{2,0,1:T(4,128)(2,1)} %all-gather.2.cloned.1.call-done) | data formatting | bytes 8388608 | tf_op jit(solution)/shard_map/all_gather | solution.py:37
  (1 shorter events, 0.0 us)
Async XLA Ops:
  7.2 1.6 copy-start
  7.2 100.8 %reduce-scatter.2.cloned.1.call-start = ((), (), s32[]{:S(2)}) async-start(), calls=%async_computation.2 | async-start | bytes 9437184 | tf_op jit(solution)/shard_map/reduce_scatter | solution.py:14
  15.6 133.2 %copy-start.1 = (f32[256,1024]{1,0:T(8,128)S(1)}, f32[256,1024]{1,0:T(8,128)}, u32[]{:S(2)}) copy-start(f32[256,1024]{1,0:T(8,128)} %param.8) | copy-start | bytes 3145732
  15.6 195.9 %all-gather.2.cloned.1.call-start = ((), (), s32[]{:S(2)}) async-start(), calls=%async_computation.3 | async-start | bytes 4718592 | tf_op jit(solution)/shard_map/all_gather | solution.py:37
Sparse Core Ops, SparseCore 0:
  15.7 92.2 reduce-scatter.1
  165.6 45.9 all-gather.1
where the time goes:
time: 224 us; the launch traced here: 223 us
  waiting for transfers between devices  135 us (60%)
  blocking collectives  49.2 us (22%)
  between operations  15.6 us (7%)
  other arithmetic  8.65 us (4%)
  local copies, waits for them, and re-layouts  7.52 us (3%)
  matrix products  6.82 us (3%)
    reduce_scatter x1, waiting for transfers between devices, on_device(): lax.psum_scatter(lax.dot_general(activations, value_grad, (((0,), (0,)),...  91.5 us
    all_gather x1, waiting for transfers between devices, on_device(): gathered = lax.all_gather(stacked, 'dp', axis=1, tiled=True)  43.7 us
    psum x1, blocking collectives, on_device(): square_sum = lax.psum(jnp.sum(grad * grad), ('dp', 'mp'))  37.9 us
    all_to_all x1, blocking collectives, on_device(): lax.all_to_all(update, 'mp', split_axis=1, concat_axis=0, tiled=True)  11.2 us
    dot_general x1, matrix products, on_device(): lax.dot_general(activations, value_grad, (((0,), (0,)), ((), ())), prefer...  6.82 us
    all_gather x1, local copies, waits for them, and re-layouts, on_device(): gathered = lax.all_gather(stacked, 'dp', axis=1, tiled=True)  4.74 us
  transfers between devices with their start and end apart: 2, of which 2 were waited for; matrix products, arithmetic and copies ran while one was open for 1% of the time, Pallas kernels for 0%

commit v1 on v0

v1 whole, which is shorter than its diff:
```python
import functools
import math

import jax
import jax.numpy as jnp
from jax import lax
from jax.experimental import pallas as pl
from jax.experimental.pallas import tpu as pltpu
from jax.sharding import PartitionSpec as P

F32 = jnp.float32
LEVELS = 32760.0
MESH = pl.DeviceIdType.MESH


def adam_terms(step):
    bias_first = 1.0 - jnp.exp(step * jnp.float32(math.log(0.9)))
    bias_second = 1.0 - jnp.exp(step * jnp.float32(math.log(0.95)))
    return 1.0 / bias_first, 1.0 / bias_second


def kernel(
    line,
    heads,
    chunks,
    clip_total,
    step_ref,
    act_ref,
    vg_ref,
    master_ref,
    first_ref,
    second_ref,
    new_master_ref,
    new_first_ref,
    new_second_ref,
    rollout_ref,
    act,
    vg,
    acc,
    q_out,
    s_out,
    q_in,
    s_in,
    norm_dp,
    norm_mp,
    w_in,
    m_in,
    v_in,
    w_out,
    m_out,
    v_out,
    update,
    in_sem,
    pair_send,
    pair_recv,
    load_sem,
    rs_send,
    rs_recv,
    norm_dp_send,
    norm_dp_recv,
    norm_mp_send,
    norm_mp_recv,
    store_sem,
    a2a_send,
    a2a_recv,
    up_send,
    down_send,
    chain_recv,
    mate_send,
    mate_recv,
):
    dpn = 2 * line
    dp = lax.axis_index("dp")
    mp = lax.axis_index("mp")
    z = dp // 2
    core = lax.rem(dp, 2)
    mate = dp + 1 - 2 * core
    tokens = act_ref.shape[0]
    rows = master_ref.shape[0]
    cols = master_ref.shape[1]
    part = rows // chunks
    head_cols = cols // heads
    tile = min(256, cols)

    barrier = pltpu.get_barrier_semaphore()
    for step in range(1, dpn):
        pl.semaphore_signal(
            barrier, inc=1, device_id={"dp": lax.rem(dp + step, dpn)}, device_id_type=MESH
        )
    for step in range(1, heads):
        pl.semaphore_signal(
            barrier, inc=1, device_id={"mp": lax.rem(mp + step, heads)}, device_id_type=MESH
        )

    lower = z < line // 2
    def owner(e):
        return jnp.where(lower, e, line - 1 - e)

    u = jnp.where(lower, z, line - 1 - z)

    def own_act(e):
        dest = owner(e)
        start = pl.multiple_of((dest * 2 + core) * rows, rows)
        return pltpu.make_async_copy(
            act_ref.at[:, pl.ds(start, rows)],
            act.at[dest, pl.ds(0, tokens)],
            in_sem.at[dest],
        )

    def own_vg():
        return pltpu.make_async_copy(vg_ref, vg.at[pl.ds(0, tokens)], in_sem.at[line])

    def pair_act(e):
        dest = owner(e)
        start = pl.multiple_of((dest * 2 + 1 - core) * rows, rows)
        return pltpu.make_async_remote_copy(
            src_ref=act_ref.at[:, pl.ds(start, rows)],
            dst_ref=act.at[dest, pl.ds(tokens, tokens)],
            send_sem=pair_send.at[dest],
            recv_sem=pair_recv.at[dest],
            device_id={"dp": mate},
            device_id_type=MESH,
        )

    def pair_vg():
        return pltpu.make_async_remote_copy(
            src_ref=vg_ref,
            dst_ref=vg.at[pl.ds(tokens, tokens)],
            send_sem=pair_send.at[line],
            recv_sem=pair_recv.at[line],
            device_id={"dp": mate},
            device_id_type=MESH,
        )

    order = list(range(line - 1, -1, -1))
    own_vg().start()
    for e in order:
        own_act(e).start()
    loads = [
        pltpu.make_async_copy(src, dst, load_sem.at[i])
        for i, (src, dst) in enumerate(
            ((master_ref, w_in), (first_ref, m_in), (second_ref, v_in))
        )
    ]
    pl.semaphore_wait(barrier, dpn - 1 + heads - 1)
    pair_act(order[0]).start()
    pair_vg().start()
    for e in order[1:]:
        pair_act(e).start()
    for copy in loads:
        copy.start()

    def multiply(e):
        dest = owner(e)
        own_act(e).wait()
        pair_act(e).wait_recv()

        @pl.loop(0, cols // tile)
        def _(n):
            at = pl.ds(pl.multiple_of(n * tile, tile), tile)
            acc[dest, :, at] = lax.dot_general(
                act[dest], vg[:, at], (((0,), (0,)), ((), ())), preferred_element_type=F32
            )

    def hop(dest, way, chunk):
        to = (z + 1 - 2 * way) * 2 + core
        data = pltpu.make_async_remote_copy(
            src_ref=q_out.at[dest, chunk],
            dst_ref=q_in.at[way, dest, chunk],
            send_sem=rs_send.at[0, dest, chunk],
            recv_sem=rs_recv.at[0, way, dest, chunk],
            device_id={"dp": to},
            device_id_type=MESH,
        )
        scale = pltpu.make_async_remote_copy(
            src_ref=s_out.at[dest, chunk],
            dst_ref=s_in.at[way, dest, chunk],
            send_sem=rs_send.at[1, dest, chunk],
            recv_sem=rs_recv.at[1, way, dest, chunk],
            device_id={"dp": to},
            device_id_type=MESH,
        )
        return data, scale

    def take(dest, way, chunk):
        for copy in hop(dest, way, chunk):
            copy.wait_recv()
        at = pl.ds(pl.multiple_of(chunk * part, part), part)
        for n in range(0, cols, tile):
            here = slice(n, n + tile)
            got = q_in[way, dest, chunk, :, here].astype(jnp.int32).astype(F32)
            acc[dest, at, here] += got * (s_in[way, dest, chunk, :, here] * (1.0 / LEVELS))

    def give(dest, way, chunk):
        at = pl.ds(pl.multiple_of(chunk * part, part), part)
        for n in range(0, cols, tile):
            here = slice(n, n + tile)
            total = acc[dest, at, here]
            top = jnp.maximum(jnp.max(jnp.abs(total), axis=0, keepdims=True), 1e-30)
            s_out[dest, chunk, :, here] = top
            q_out[dest, chunk, :, here] = (
                jnp.round(total * (LEVELS / top)).astype(jnp.int32).astype(jnp.int16)
            )
        for copy in hop(dest, way, chunk):
            copy.start()

    forward = jnp.where(lower, 0, 1)
    backward = 1 - forward

    def pass_forward(k):
        e = line - 1 - k
        dest = owner(e)

        @pl.when(u < e)
        def _():
            @pl.loop(0, chunks)
            def _(chunk):
                @pl.when(u > 0)
                def _():
                    take(dest, forward, chunk)

                give(dest, forward, chunk)

    def pass_backward(k):
        dest = owner(k)

        @pl.when(u > k)
        def _():
            @pl.loop(0, chunks)
            def _(chunk):
                take(dest, backward, chunk)
                give(dest, backward, chunk)

    own_vg().wait()
    pair_vg().wait_recv()
    multiply(order[0])
    pass_forward(0)
    for e in order[1:]:
        multiply(e)
    for k in range(1, line - 1):
        pass_forward(k)
        if k - 1 < line // 2 - 1:
            pass_backward(k - 1)

    norm_dp[dp] = jnp.zeros(norm_dp.shape[1:], F32)

    @pl.loop(0, chunks)
    def _(chunk):
        @pl.when(u > 0)
        def _():
            take(z, forward, chunk)

        take(z, backward, chunk)
        at = pl.ds(pl.multiple_of(chunk * part, part), part)
        for n in range(0, cols, tile):
            grad = acc[z, at, slice(n, n + tile)]
            square = jnp.sum((grad * grad).reshape(part // 8, 8, tile), axis=0)
            for lane in range(0, tile, 128):
                norm_dp[dp] += square[:, lane : lane + 128]

    def norm_to_dp(step):
        return pltpu.make_async_remote_copy(
            src_ref=norm_dp.at[dp],
            dst_ref=norm_dp.at[dp],
            send_sem=norm_dp_send.at[step],
            recv_sem=norm_dp_recv.at[step],
            device_id={"dp": lax.rem(dp + step, dpn)},
            device_id_type=MESH,
        )

    def norm_to_mp(step):
        return pltpu.make_async_remote_copy(
            src_ref=norm_mp.at[mp],
            dst_ref=norm_mp.at[mp],
            send_sem=norm_mp_send.at[step],
            recv_sem=norm_mp_recv.at[step],
            device_id={"mp": lax.rem(mp + step, heads)},
            device_id_type=MESH,
        )

    for step in range(1, dpn):
        norm_to_dp(step).start()
    for copy in loads:
        copy.wait()
    for step in range(1, dpn):
        norm_to_dp(step).wait_recv()
    norm_mp[mp] = jnp.sum(norm_dp[...], axis=0)
    for step in range(1, heads):
        norm_to_mp(step).start()
    for step in range(1, heads):
        norm_to_mp(step).wait_recv()
    square_sum = jnp.sum(jnp.sum(norm_mp[...], axis=0), keepdims=True)
    factor = jnp.minimum(1.0, clip_total / (jnp.sqrt(square_sum) + 1e-06))
    step_count = jnp.full((1, 1), step_ref[0].astype(F32), F32)
    scale_first, scale_second = adam_terms(step_count)

    def block(head, origin):
        return rollout_ref.at[pl.ds(pl.multiple_of((head * dpn + origin) * rows, rows), rows)]

    mine = pltpu.make_async_copy(update.at[mp], block(mp, dp), store_sem.at[3])

    def to_head(step):
        head = lax.rem(mp + step, heads)
        return pltpu.make_async_remote_copy(
            src_ref=update.at[head],
            dst_ref=block(mp, dp),
            send_sem=a2a_send.at[step],
            recv_sem=a2a_recv.at[step],
            device_id={"mp": head},
            device_id_type=MESH,
        )

    def relay(source, head, at_z, send, recv, to):
        return pltpu.make_async_remote_copy(
            src_ref=source,
            dst_ref=block(head, at_z * 2 + core),
            send_sem=send.at[at_z, head],
            recv_sem=recv.at[at_z, head],
            device_id={"dp": to},
            device_id_type=MESH,
        )

    def send_up(source, head, at_z):
        return relay(source, head, at_z, up_send, chain_recv, dp + 2)

    def send_down(source, head, at_z):
        return relay(source, head, at_z, down_send, chain_recv, dp - 2)

    def send_mate(source, head, at_z):
        return relay(source, head, at_z, mate_send, mate_recv, mate)

    def spread(source, head):
        @pl.when(z < line - 1)
        def _():
            send_up(source, head, z).start()

        @pl.when(z > 0)
        def _():
            send_down(source, head, z).start()

        send_mate(source, head, z).start()

    slab = min(32, rows)
    for step in range(heads):
        head = lax.rem(mp + step, heads)
        lanes = pl.ds(pl.multiple_of(head * head_cols, head_cols), head_cols)

        @pl.loop(0, rows // slab)
        def _(r):
            at = pl.ds(pl.multiple_of(r * slab, slab), slab)
            clipped = acc[z, at, lanes] * factor
            weight = w_in[at, lanes]
            first = 0.9 * m_in[at, lanes] + 0.1 * clipped
            second = 0.95 * v_in[at, lanes] + 0.05 * clipped * clipped
            m_out[at, lanes] = first
            v_out[at, lanes] = second
            direction = (first * scale_first) / (
                jnp.sqrt(second * scale_second) + 1e-08
            ) + 0.1 * weight
            w_out[at, lanes] = weight - 0.01 * direction
            update[head, at, :] = direction.astype(jnp.bfloat16)

        if step == 0:
            mine.start()
            spread(update.at[mp], mp)
        else:
            to_head(step).start()

    stores = [
        pltpu.make_async_copy(src, dst, store_sem.at[i])
        for i, (src, dst) in enumerate(
            ((w_out, new_master_ref), (m_out, new_first_ref), (v_out, new_second_ref))
        )
    ]
    for copy in stores:
        copy.start()

    for step in range(1, heads):
        head = lax.rem(mp + heads - step, heads)
        to_head(step).wait_recv()
        spread(block(head, dp), head)

    for far in range(1, line):
        for step in range(heads):
            head = lax.rem(mp + heads - step, heads)

            @pl.when(z - far >= 0)
            def _():
                at_z = z - far
                source = block(head, at_z * 2 + core)
                send_up(source, head, at_z).wait_recv()

                @pl.when(z < line - 1)
                def _():
                    send_up(source, head, at_z).start()

                send_mate(source, head, at_z).start()

            @pl.when(z + far < line)
            def _():
                at_z = z + far
                source = block(head, at_z * 2 + core)
                send_down(source, head, at_z).wait_recv()

                @pl.when(z > 0)
                def _():
                    send_down(source, head, at_z).start()

                send_mate(source, head, at_z).start()

    for at_z in range(line):
        for head in range(heads):
            source = block(head, at_z * 2 + core)
            send_mate(source, head, at_z).wait_recv()
            send_mate(source, head, at_z).wait_send()

            @pl.when((z < line - 1) & (z >= at_z))
            def _():
                send_up(source, head, at_z).wait_send()

            @pl.when((z > 0) & (z <= at_z))
            def _():
                send_down(source, head, at_z).wait_send()

    for step in range(1, heads):
        to_head(step).wait_send()
        norm_to_mp(step).wait_send()
    for step in range(1, dpn):
        norm_to_dp(step).wait_send()
    for dest in range(line):
        pair_act(dest).wait_send()

        @pl.when(z != dest)
        def _():
            @pl.loop(0, chunks)
            def _(chunk):
                for copy in hop(dest, 0, chunk):
                    copy.wait_send()

    pair_vg().wait_send()
    mine.wait()
    for copy in stores:
        copy.wait()


def one_kernel(line, heads, activations, value_grad, master, first_moment, second_moment, step_count):
    rows, cols = master.shape
    tokens = activations.shape[0]
    chunks = 4
    part = rows // chunks
    dpn = 2 * line
    clip_total = 0.5 * math.sqrt(rows * dpn * heads * cols)
    hbm = pl.BlockSpec(memory_space=pl.ANY)
    owned = jax.ShapeDtypeStruct((rows, cols), F32)
    wide = pltpu.VMEM((rows, cols), F32)
    dma = pltpu.SemaphoreType.DMA
    return pl.pallas_call(
        functools.partial(kernel, line, heads, chunks, clip_total),
        out_shape=(
            owned,
            owned,
            owned,
            jax.ShapeDtypeStruct((rows * dpn * heads, cols // heads), jnp.bfloat16),
        ),
        in_specs=[pl.BlockSpec(memory_space=pltpu.SMEM)] + [hbm] * 5,
        out_specs=(hbm,) * 4,
        scratch_shapes=[
            pltpu.VMEM((line, 2 * tokens, rows), jnp.bfloat16),
            pltpu.VMEM((2 * tokens, cols), jnp.bfloat16),
            pltpu.VMEM((line, rows, cols), F32),
            pltpu.VMEM((line, chunks, part, cols), jnp.int16),
            pltpu.VMEM((line, chunks, 1, cols), F32),
            pltpu.VMEM((2, line, chunks, part, cols), jnp.int16),
            pltpu.VMEM((2, line, chunks, 1, cols), F32),
            pltpu.VMEM((dpn, 8, 128), F32),
            pltpu.VMEM((heads, 8, 128), F32),
            wide,
            wide,
            wide,
            wide,
            wide,
            wide,
            pltpu.VMEM((heads, rows, cols // heads), jnp.bfloat16),
            dma((line + 1,)),
            dma((line + 1,)),
            dma((line + 1,)),
            dma((3,)),
            dma((2, line, chunks)),
            dma((2, 2, line, chunks)),
            dma((dpn,)),
            dma((dpn,)),
            dma((heads,)),
            dma((heads,)),
            dma((4,)),
            dma((heads,)),
            dma((heads,)),
            dma((line, heads)),
            dma((line, heads)),
            dma((line, heads)),
            dma((line, heads)),
            dma((line, heads)),
        ],
        compiler_params=pltpu.CompilerParams(
            collective_id=0, has_side_effects=True, vmem_limit_bytes=48 * 1024 * 1024
        ),
    )(step_count, activations, value_grad, master, first_moment, second_moment)


def plain(activations, value_grad, master, first_moment, second_moment, step_count):
    own_rows, cols = master.shape
    grad = lax.psum_scatter(
        lax.dot_general(
            activations, value_grad, (((0,), (0,)), ((), ())), preferred_element_type=F32
        ),
        "dp",
        scatter_dimension=0,
        tiled=True,
    )
    square_sum = lax.psum(jnp.sum(grad * grad), ("dp", "mp"))
    head_count = lax.axis_size("mp")
    clip_total = 0.5 * math.sqrt(own_rows * lax.axis_size("dp") * head_count * cols)
    factor = jnp.minimum(jnp.float32(1.0), clip_total / (jnp.sqrt(square_sum) + 1e-06))
    clipped = factor * grad
    new_first = 0.9 * first_moment + 0.1 * clipped
    new_second = 0.95 * second_moment + 0.05 * clipped * clipped
    scale_first, scale_second = adam_terms(step_count[0].astype(F32))
    direction = new_first * scale_first / (jnp.sqrt(new_second * scale_second) + 1e-08) + 0.1 * master
    new_master = master - 0.01 * direction
    update = direction.astype(jnp.bfloat16)
    received = lax.all_to_all(update, "mp", split_axis=1, concat_axis=0, tiled=True)
    stacked = received.reshape(head_count, own_rows, received.shape[1])
    gathered = lax.all_gather(stacked, "dp", axis=1, tiled=True)
    return (new_master, new_first, new_second, gathered.reshape(-1, gathered.shape[2]))


def solution(mesh):
    dpn, heads = mesh.shape["dp"], mesh.shape["mp"]

    def on_device(*args):
        rows, cols = args[2].shape
        if dpn % 4 == 0 and dpn <= 16 and rows % 128 == 0 and (cols // heads) % 128 == 0:
            return one_kernel(dpn // 2, heads, *args)
        return plain(*args)

    in_specs = (
        P("dp", "mp"),
        P("dp", None),
        P(("mp", "dp"), None),
        P(("mp", "dp"), None),
        P(("mp", "dp"), None),
        P(),
    )
    out_specs = (P(("mp", "dp"), None), P(("mp", "dp"), None), P(("mp", "dp"), None), P(None, "mp"))
    return jax.shard_map(
        on_device, mesh=mesh, in_specs=in_specs, out_specs=out_specs, check_vma=False
    )
```

time: 224 us -> 107 us (0.48)
  waiting for transfers between devices: 135 us -> 0 us
  Pallas kernels: 0 us -> 97.6 us
  blocking collectives: 49.2 us -> 0 us
  between operations: 15.6 us -> 1.31 us
  other arithmetic: 8.65 us -> 0 us
  matrix products: 6.82 us -> 0 us
    pallas_call x0 -> x1, Pallas kernels: none -> 97.6 us  [one_kernel(): pl.pallas_call(functools.partial(kernel, line, heads, chunks, clip_total)...]
    reduce_scatter x1 -> x0, waiting for transfers between devices: 91.5 us -> none  [on_device(): lax.psum_scatter(lax.dot_general(activations, value_grad, (((0,), (0,)),...]
    all_gather x1 -> x0, waiting for transfers between devices: 43.7 us -> none  [on_device(): gathered = lax.all_gather(stacked, 'dp', axis=1, tiled=True)]
    psum x1 -> x0, blocking collectives: 37.9 us -> none  [on_device(): square_sum = lax.psum(jnp.sum(grad * grad), ('dp', 'mp'))]
    all_to_all x1 -> x0, blocking collectives: 11.2 us -> none  [on_device(): lax.all_to_all(update, 'mp', split_axis=1, concat_axis=0, tiled=True)]
    dot_general x1 -> x0, matrix products: 6.82 us -> none  [on_device(): lax.dot_general(activations, value_grad, (((0,), (0,)), ((), ())), prefer...]
    unnamed x4 -> x10, local copies, waits for them, and re-layouts: 1.55 us -> 7.51 us
    all_gather x1 -> x0, local copies, waits for them, and re-layouts: 4.74 us -> none  [on_device(): gathered = lax.all_gather(stacked, 'dp', axis=1, tiled=True)]
  transfers between devices with their start and end apart: 2 -> 0, of which waited for: 2 -> 0; matrix products, arithmetic and copies ran while one was open for 1% -> 0% of each run, Pallas kernels for 0% -> 0%
where the time goes in v1:
time: 107 us; the launch traced here: 106 us
  Pallas kernels  97.6 us (91%)
  local copies, waits for them, and re-layouts  7.51 us (7%)
  between operations  1.31 us (1%)
    pallas_call x1, Pallas kernels, one_kernel(): pl.pallas_call(functools.partial(kernel, line, heads, chunks, clip_total)...  97.6 us
    unnamed x10, local copies, waits for them, and re-layouts  7.51 us

profile of v1, /device:TPU:0, one launch (start us, length us, event | category | flops | bytes accessed | tf_op | source)
XLA Modules:
  0.0 106.4 jit_solution(10088626417071482199)
XLA Ops:
  1.3 0.0 copy-start
  1.3 1.2 %copy-done = bf16[512,1024]{1,0:T(8,128)(2,1)S(1)} copy-done((bf16[512,1024]{1,0:T(8,128)(2,1)S(1)}, bf16[512,1024]{1,0:T(8,128)(2,1)}, u32[]{:S(2)}) %copy-start) | copy-done | bytes 1048600
  2.5 0.0 copy-start.1
  2.5 1.2 %copy-done.1 = f32[256,1024]{1,0:T(8,128)S(1)} copy-done((f32[256,1024]{1,0:T(8,128)S(1)}, f32[256,1024]{1,0:T(8,128)}, u32[]{:S(2)}) %copy-start.1) | copy-done | bytes 1048600
  3.7 97.6 %shard_map.93 = (f32[256,1024]{1,0:T(8,128)S(1)}, f32[256,1024]{1,0:T(8,128)S(1)}, f32[256,1024]{1,0:T(8,128)S(1)}, bf16[8192,256]{1,0:T(8,128)(2,1)}) custom-call(s32[1]{0:T(128)S(6)} %copy.14.step_ref, bf16[512,2048]{1,0:T(8,128)(2,1)} %act_ref.1, bf16[512,1024]{1,0:T(8,128)(2,1)S(1)} %copy-done, f32[256,1024]{1,0:T(8,128)S(1)} %copy-done.1, ...), custom_call_target="tpu_custom_call" | custom-call | tf_op jit(solution)/shard_map/pallas_call | solution.py:457
  101.3 0.0 copy-start.2
  101.3 1.0 copy.15
  102.3 1.0 copy.16
  103.3 1.0 copy.17
  104.2 0.1 copy-done.2
  104.4 2.0 %copy.18 = bf16[8192,256]{1,0:T(8,128)(2,1)} copy(bf16[8192,256]{1,0:T(8,128)(2,1)S(1)} %copy-done.2) | data formatting | bytes 8388608
Async XLA Ops:
  1.3 1.2 %copy-start = (bf16[512,1024]{1,0:T(8,128)(2,1)S(1)}, bf16[512,1024]{1,0:T(8,128)(2,1)}, u32[]{:S(2)}) copy-start(bf16[512,1024]{1,0:T(8,128)(2,1)} %vg_ref.1) | copy-start | bytes 3145732
  2.5 1.2 %copy-start.1 = (f32[256,1024]{1,0:T(8,128)S(1)}, f32[256,1024]{1,0:T(8,128)}, u32[]{:S(2)}) copy-start(f32[256,1024]{1,0:T(8,128)} %master_ref.1) | copy-start | bytes 3145732
  101.3 3.1 %copy-start.2 = (bf16[8192,256]{1,0:T(8,128)(2,1)S(1)}, bf16[8192,256]{1,0:T(8,128)(2,1)}, u32[]{:S(2)}) copy-start(bf16[8192,256]{1,0:T(8,128)(2,1)} %get-tuple-element.11) | copy-start | bytes 12582916

commit v2 on v1

--- a/solution.py
+++ b/solution.py
@@ -10,6 +10,7 @@
 
 F32 = jnp.float32
 LEVELS = 32760.0
+PIECES = (1, 1, 1, 4)
 MESH = pl.DeviceIdType.MESH
 
 
@@ -78,9 +79,9 @@
     tokens = act_ref.shape[0]
     rows = master_ref.shape[0]
     cols = master_ref.shape[1]
-    part = rows // chunks
+    tile = cols // chunks
+    group = rows // 8
     head_cols = cols // heads
-    tile = min(256, cols)
 
     barrier = pltpu.get_barrier_semaphore()
     for step in range(1, dpn):
@@ -107,8 +108,11 @@
             in_sem.at[dest],
         )
 
-    def own_vg():
-        return pltpu.make_async_copy(vg_ref, vg.at[pl.ds(0, tokens)], in_sem.at[line])
+    def own_vg(n):
+        at = slice(n * tile, (n + 1) * tile)
+        return pltpu.make_async_copy(
+            vg_ref.at[:, at], vg.at[pl.ds(0, tokens), at], in_sem.at[line + n]
+        )
 
     def pair_act(e):
         dest = owner(e)
@@ -122,19 +126,22 @@
             device_id_type=MESH,
         )
 
-    def pair_vg():
+    def pair_vg(n):
+        at = slice(n * tile, (n + 1) * tile)
         return pltpu.make_async_remote_copy(
-            src_ref=vg_ref,
-            dst_ref=vg.at[pl.ds(tokens, tokens)],
-            send_sem=pair_send.at[line],
-            recv_sem=pair_recv.at[line],
+            src_ref=vg_ref.at[:, at],
+            dst_ref=vg.at[pl.ds(tokens, tokens), at],
+            send_sem=pair_send.at[line + n],
+            recv_sem=pair_recv.at[line + n],
             device_id={"dp": mate},
             device_id_type=MESH,
         )
 
     order = list(range(line - 1, -1, -1))
-    own_vg().start()
-    for e in order:
+    own_act(order[0]).start()
+    for n in range(chunks):
+        own_vg(n).start()
+    for e in order[1:]:
         own_act(e).start()
     loads = [
         pltpu.make_async_copy(src, dst, load_sem.at[i])
@@ -144,23 +151,18 @@
     ]
     pl.semaphore_wait(barrier, dpn - 1 + heads - 1)
     pair_act(order[0]).start()
-    pair_vg().start()
+    for n in range(chunks):
+        pair_vg(n).start()
     for e in order[1:]:
         pair_act(e).start()
     for copy in loads:
         copy.start()
 
-    def multiply(e):
-        dest = owner(e)
-        own_act(e).wait()
-        pair_act(e).wait_recv()
-
-        @pl.loop(0, cols // tile)
-        def _(n):
-            at = pl.ds(pl.multiple_of(n * tile, tile), tile)
-            acc[dest, :, at] = lax.dot_general(
-                act[dest], vg[:, at], (((0,), (0,)), ((), ())), preferred_element_type=F32
-            )
+    def multiply(dest, n):
+        at = pl.ds(pl.multiple_of(n * tile, tile), tile)
+        acc[dest, :, at] = lax.dot_general(
+            act[dest], vg[:, at], (((0,), (0,)), ((), ())), preferred_element_type=F32
+        )
 
     def hop(dest, way, chunk):
         to = (z + 1 - 2 * way) * 2 + core
@@ -185,20 +187,21 @@
     def take(dest, way, chunk):
         for copy in hop(dest, way, chunk):
             copy.wait_recv()
-        at = pl.ds(pl.multiple_of(chunk * part, part), part)
-        for n in range(0, cols, tile):
-            here = slice(n, n + tile)
-            got = q_in[way, dest, chunk, :, here].astype(jnp.int32).astype(F32)
-            acc[dest, at, here] += got * (s_in[way, dest, chunk, :, here] * (1.0 / LEVELS))
+        lanes = pl.ds(pl.multiple_of(chunk * tile, tile), tile)
+        for g in range(8):
+            here = slice(g * group, (g + 1) * group)
+            got = q_in[way, dest, chunk, here, :].astype(jnp.int32).astype(F32)
+            top = s_in[way, dest, chunk, slice(g, g + 1), :]
+            acc[dest, here, lanes] += got * (top * (1.0 / LEVELS))
 
     def give(dest, way, chunk):
-        at = pl.ds(pl.multiple_of(chunk * part, part), part)
-        for n in range(0, cols, tile):
-            here = slice(n, n + tile)
-            total = acc[dest, at, here]
+        lanes = pl.ds(pl.multiple_of(chunk * tile, tile), tile)
+        for g in range(8):
+            here = slice(g * group, (g + 1) * group)
+            total = acc[dest, here, lanes]
             top = jnp.maximum(jnp.max(jnp.abs(total), axis=0, keepdims=True), 1e-30)
-            s_out[dest, chunk, :, here] = top
-            q_out[dest, chunk, :, here] = (
+            s_out[dest, chunk, slice(g, g + 1), :] = top
+            q_out[dest, chunk, here, :] = (
                 jnp.round(total * (LEVELS / top)).astype(jnp.int32).astype(jnp.int16)
             )
         for copy in hop(dest, way, chunk):
@@ -231,12 +234,30 @@
                 take(dest, backward, chunk)
                 give(dest, backward, chunk)
 
-    own_vg().wait()
-    pair_vg().wait_recv()
-    multiply(order[0])
-    pass_forward(0)
+    far = owner(line - 1)
+    own_act(line - 1).wait()
+    pair_act(line - 1).wait_recv()
+    for n in range(chunks):
+        own_vg(n).wait()
+        pair_vg(n).wait_recv()
+        multiply(far, n)
+
+        @pl.when(u == 0)
+        def _():
+            give(far, forward, n)
+
     for e in order[1:]:
-        multiply(e)
+        own_act(e).wait()
+        pair_act(e).wait_recv()
+
+        @pl.loop(0, chunks)
+        def _(n):
+            multiply(owner(e), n)
+
+    @pl.when(u > 0)
+    def _():
+        pass_forward(0)
+
     for k in range(1, line - 1):
         pass_forward(k)
         if k - 1 < line // 2 - 1:
@@ -251,12 +272,13 @@
             take(z, forward, chunk)
 
         take(z, backward, chunk)
-        at = pl.ds(pl.multiple_of(chunk * part, part), part)
-        for n in range(0, cols, tile):
-            grad = acc[z, at, slice(n, n + tile)]
-            square = jnp.sum((grad * grad).reshape(part // 8, 8, tile), axis=0)
-            for lane in range(0, tile, 128):
-                norm_dp[dp] += square[:, lane : lane + 128]
+        lanes = pl.ds(pl.multiple_of(chunk * tile, tile), tile)
+        square = jnp.zeros((8, tile), F32)
+        for g in range(8):
+            grad = acc[z, slice(g * group, (g + 1) * group), lanes]
+            square += jnp.sum((grad * grad).reshape(group // 8, 8, tile), axis=0)
+        for lane in range(0, tile, 128):
+            norm_dp[dp] += square[:, lane : lane + 128]
 
     def norm_to_dp(step):
         return pltpu.make_async_remote_copy(
@@ -341,7 +363,7 @@
         send_mate(source, head, z).start()
 
     slab = min(32, rows)
-    for step in range(heads):
+    for step in (*range(1, heads), 0):
         head = lax.rem(mp + step, heads)
         lanes = pl.ds(pl.multiple_of(head * head_cols, head_cols), head_cols)
 
@@ -437,9 +459,28 @@
                 for copy in hop(dest, 0, chunk):
                     copy.wait_send()
 
-    pair_vg().wait_send()
+    for n in range(chunks):
+        pair_vg(n).wait_send()
     mine.wait()
     for copy in stores:
+        copy.wait()
+
+
+def settle(*refs):
+    count = (len(refs) - 1) // 2
+    sem = refs[-1]
+    copies = []
+    for i in range(count):
+        source, place = refs[i], refs[count + i]
+        piece = source.shape[0] // PIECES[i]
+        for j in range(PIECES[i]):
+            at = pl.ds(j * piece, piece)
+            copies.append(
+                pltpu.make_async_copy(source.at[at], place.at[at], sem.at[len(copies)])
+            )
+    for copy in copies:
+        copy.start()
+    for copy in copies:
         copy.wait()
 
 
@@ -447,14 +488,13 @@
     rows, cols = master.shape
     tokens = activations.shape[0]
     chunks = 4
-    part = rows // chunks
     dpn = 2 * line
     clip_total = 0.5 * math.sqrt(rows * dpn * heads * cols)
     hbm = pl.BlockSpec(memory_space=pl.ANY)
     owned = jax.ShapeDtypeStruct((rows, cols), F32)
     wide = pltpu.VMEM((rows, cols), F32)
     dma = pltpu.SemaphoreType.DMA
-    return pl.pallas_call(
+    results = pl.pallas_call(
         functools.partial(kernel, line, heads, chunks, clip_total),
         out_shape=(
             owned,
@@ -462,16 +502,17 @@
             owned,
             jax.ShapeDtypeStruct((rows * dpn * heads, cols // heads), jnp.bfloat16),
         ),
-        in_specs=[pl.BlockSpec(memory_space=pltpu.SMEM)] + [hbm] * 5,
+        in_specs=[pl.BlockSpec(memory_space=pltpu.SMEM)]
+        + [hbm] * 5,
         out_specs=(hbm,) * 4,
         scratch_shapes=[
             pltpu.VMEM((line, 2 * tokens, rows), jnp.bfloat16),
             pltpu.VMEM((2 * tokens, cols), jnp.bfloat16),
             pltpu.VMEM((line, rows, cols), F32),
-            pltpu.VMEM((line, chunks, part, cols), jnp.int16),
-            pltpu.VMEM((line, chunks, 1, cols), F32),
-            pltpu.VMEM((2, line, chunks, part, cols), jnp.int16),
-            pltpu.VMEM((2, line, chunks, 1, cols), F32),
+            pltpu.VMEM((line, chunks, rows, cols // chunks), jnp.int16),
+            pltpu.VMEM((line, chunks, 8, cols // chunks), F32),
+            pltpu.VMEM((2, line, chunks, rows, cols // chunks), jnp.int16),
+            pltpu.VMEM((2, line, chunks, 8, cols // chunks), F32),
             pltpu.VMEM((dpn, 8, 128), F32),
             pltpu.VMEM((heads, 8, 128), F32),
             wide,
@@ -481,9 +522,9 @@
             wide,
             wide,
             pltpu.VMEM((heads, rows, cols // heads), jnp.bfloat16),
-            dma((line + 1,)),
-            dma((line + 1,)),
-            dma((line + 1,)),
+            dma((line + chunks,)),
+            dma((line + chunks,)),
+            dma((line + chunks,)),
             dma((3,)),
             dma((2, line, chunks)),
             dma((2, 2, line, chunks)),
@@ -501,9 +542,24 @@
             dma((line, heads)),
         ],
         compiler_params=pltpu.CompilerParams(
-            collective_id=0, has_side_effects=True, vmem_limit_bytes=48 * 1024 * 1024
+            collective_id=0, has_side_effects=True, vmem_limit_bytes=28 * 1024 * 1024
         ),
-    )(step_count, activations, value_grad, master, first_moment, second_moment)
+    )(
+        step_count,
+        *(
+            pltpu.with_memory_space_constraint(x, pltpu.HBM)
+            for x in (activations, value_grad, master, first_moment, second_moment)
+        ),
+    )
+    shapes = tuple(jax.ShapeDtypeStruct(x.shape, x.dtype) for x in results)
+    return pl.pallas_call(
+        settle,
+        out_shape=shapes,
+        in_specs=[hbm] * 4,
+        out_specs=(hbm,) * 4,
+        scratch_shapes=[dma((sum(PIECES),))],
+        compiler_params=pltpu.CompilerParams(vmem_limit_bytes=4 * 1024 * 1024),
+    )(*(pltpu.with_memory_space_constraint(x, pltpu.VMEM) for x in results))
 
 
 def plain(activations, value_grad, master, first_moment, second_moment, step_count):

time: 107 us -> 100 us (0.935)
  local copies, waits for them, and re-layouts: 7.51 us -> 0 us
    unnamed x10 -> x0, local copies, waits for them, and re-layouts: 7.51 us -> none
    pallas_call x0 -> x1, Pallas kernels: none -> 3.05 us  [one_kernel(): pl.pallas_call(settle, out_shape=shapes, in_specs=[hbm] * 4, out_specs=(h...]
    pallas_call x1, Pallas kernels: 97.6 us -> 95.6 us  [one_kernel(): pl.pallas_call(functools.partial(kernel, line, heads, chunks, clip_total)...]
where the time goes in v2:
time: 100 us; the launch traced here: 99.9 us
  Pallas kernels  98.6 us (99%)
  between operations  1.29 us (1%)
    pallas_call x1, Pallas kernels, one_kernel(): pl.pallas_call(functools.partial(kernel, line, heads, chunks, clip_total)...  95.6 us
    pallas_call x1, Pallas kernels, one_kernel(): pl.pallas_call(settle, out_shape=shapes, in_specs=[hbm] * 4, out_specs=(h...  3.05 us

profile of v2, /device:TPU:0, one launch (start us, length us, event | category | flops | bytes accessed | tf_op | source)
XLA Modules:
  0.0 99.9 jit_solution(9082235905386180888)
XLA Ops:
  1.3 95.6 %shard_map.93 = (f32[256,1024]{1,0:T(8,128)S(1)}, f32[256,1024]{1,0:T(8,128)S(1)}, f32[256,1024]{1,0:T(8,128)S(1)}, bf16[8192,256]{1,0:T(8,128)(2,1)S(1)}) custom-call(s32[1]{0:T(128)S(6)} %copy.10.step_ref, bf16[512,2048]{1,0:T(8,128)(2,1)} %act_ref.1, bf16[512,1024]{1,0:T(8,128)(2,1)} %vg_ref.1, f32[256,1024]{1,0:T(8,128)} %master_ref.1, ...), custom_call_target="tpu_custom_call" | custom-call | tf_op jit(solution)/shard_map/pallas_call | solution.py:497
  96.9 3.0 %shard_map.94 = (f32[256,1024]{1,0:T(8,128)}, f32[256,1024]{1,0:T(8,128)}, f32[256,1024]{1,0:T(8,128)}, bf16[8192,256]{1,0:T(8,128)(2,1)}) custom-call(f32[256,1024]{1,0:T(8,128)S(1)} %get-tuple-element.8.refs_0_, f32[256,1024]{1,0:T(8,128)S(1)} %get-tuple-element.9.refs_1_, f32[256,1024]{1,0:T(8,128)S(1)} %get-tuple-element.10.refs_2_, ...), custom_call_target="tpu_custom_call" | custom-call | tf_op jit(solution)/shard_map/pallas_call | solution.py:555

commit v3 on v2

--- a/solution.py
+++ b/solution.py
@@ -188,21 +188,25 @@
         for copy in hop(dest, way, chunk):
             copy.wait_recv()
         lanes = pl.ds(pl.multiple_of(chunk * tile, tile), tile)
+        top = s_in[way, dest, chunk] * (1.0 / LEVELS)
         for g in range(8):
             here = slice(g * group, (g + 1) * group)
             got = q_in[way, dest, chunk, here, :].astype(jnp.int32).astype(F32)
-            top = s_in[way, dest, chunk, slice(g, g + 1), :]
-            acc[dest, here, lanes] += got * (top * (1.0 / LEVELS))
+            acc[dest, here, lanes] += got * top
 
     def give(dest, way, chunk):
         lanes = pl.ds(pl.multiple_of(chunk * tile, tile), tile)
+        peak = jnp.zeros((8, tile), F32)
+        for g in range(rows // 8):
+            peak = jnp.maximum(peak, jnp.abs(acc[dest, slice(g * 8, (g + 1) * 8), lanes]))
+        top = jnp.maximum(jnp.max(peak, axis=0, keepdims=True), 1e-30)
+        s_out[dest, chunk] = top
+        ratio = LEVELS / top
         for g in range(8):
             here = slice(g * group, (g + 1) * group)
             total = acc[dest, here, lanes]
-            top = jnp.maximum(jnp.max(jnp.abs(total), axis=0, keepdims=True), 1e-30)
-            s_out[dest, chunk, slice(g, g + 1), :] = top
             q_out[dest, chunk, here, :] = (
-                jnp.round(total * (LEVELS / top)).astype(jnp.int32).astype(jnp.int16)
+                jnp.round(total * ratio).astype(jnp.int32).astype(jnp.int16)
             )
         for copy in hop(dest, way, chunk):
             copy.start()
@@ -267,11 +271,12 @@
 
     @pl.loop(0, chunks)
     def _(chunk):
+        take(z, backward, chunk)
+
         @pl.when(u > 0)
         def _():
             take(z, forward, chunk)
 
-        take(z, backward, chunk)
         lanes = pl.ds(pl.multiple_of(chunk * tile, tile), tile)
         square = jnp.zeros((8, tile), F32)
         for g in range(8):
@@ -510,9 +515,9 @@
             pltpu.VMEM((2 * tokens, cols), jnp.bfloat16),
             pltpu.VMEM((line, rows, cols), F32),
             pltpu.VMEM((line, chunks, rows, cols // chunks), jnp.int16),
-            pltpu.VMEM((line, chunks, 8, cols // chunks), F32),
+            pltpu.VMEM((line, chunks, 1, cols // chunks), F32),
             pltpu.VMEM((2, line, chunks, rows, cols // chunks), jnp.int16),
-            pltpu.VMEM((2, line, chunks, 8, cols // chunks), F32),
+            pltpu.VMEM((2, line, chunks, 1, cols // chunks), F32),
             pltpu.VMEM((dpn, 8, 128), F32),
             pltpu.VMEM((heads, 8, 128), F32),
             wide,

time: 100 us -> 98.3 us (0.983)
  Pallas kernels: 98.6 us -> 96.9 us
    pallas_call x1, Pallas kernels: 95.6 us -> 93.8 us  [one_kernel(): pl.pallas_call(functools.partial(kernel, line, heads, chunks, clip_total)...]
where the time goes in v3:
time: 98.3 us; the launch traced here: 98.2 us
  Pallas kernels  96.9 us (99%)
  between operations  1.29 us (1%)
    pallas_call x1, Pallas kernels, one_kernel(): pl.pallas_call(functools.partial(kernel, line, heads, chunks, clip_total)...  93.8 us
    pallas_call x1, Pallas kernels, one_kernel(): pl.pallas_call(settle, out_shape=shapes, in_specs=[hbm] * 4, out_specs=(h...  3.05 us

profile of v3, /device:TPU:0, one launch (start us, length us, event | category | flops | bytes accessed | tf_op | source)
XLA Modules:
  0.0 98.2 jit_solution(4206466143663714833)
XLA Ops:
  1.3 93.8 %shard_map.93 = (f32[256,1024]{1,0:T(8,128)S(1)}, f32[256,1024]{1,0:T(8,128)S(1)}, f32[256,1024]{1,0:T(8,128)S(1)}, bf16[8192,256]{1,0:T(8,128)(2,1)S(1)}) custom-call(s32[1]{0:T(128)S(6)} %copy.10.step_ref, bf16[512,2048]{1,0:T(8,128)(2,1)} %act_ref.1, bf16[512,1024]{1,0:T(8,128)(2,1)} %vg_ref.1, f32[256,1024]{1,0:T(8,128)} %master_ref.1, ...), custom_call_target="tpu_custom_call" | custom-call | tf_op jit(solution)/shard_map/pallas_call | solution.py:502
  95.1 3.0 %shard_map.94 = (f32[256,1024]{1,0:T(8,128)}, f32[256,1024]{1,0:T(8,128)}, f32[256,1024]{1,0:T(8,128)}, bf16[8192,256]{1,0:T(8,128)(2,1)}) custom-call(f32[256,1024]{1,0:T(8,128)S(1)} %get-tuple-element.8.refs_0_, f32[256,1024]{1,0:T(8,128)S(1)} %get-tuple-element.9.refs_1_, f32[256,1024]{1,0:T(8,128)S(1)} %get-tuple-element.10.refs_2_, ...), custom_call_target="tpu_custom_call" | custom-call | tf_op jit(solution)/shard_map/pallas_call | solution.py:560
